TPU v7x, 32 devices: a whole 2x2x4 slice. The times are simulated.
32 devices in a mesh: expert: 16 (over z, y, x), tok: 2 (over core).
Axes of the slice: x: 2, y: 2, z: 4, core: 2. Of those that a mesh axis runs over, the one named last changes fastest.
Arguments:
- tokens: bfloat16 [2048, 3584], P(('expert', 'tok')), may hold values from -6 to 6
- routes: int32 [2048, 8], P(('expert', 'tok')), may hold values from 0 to 15, all different within a row; in each aligned block of 64 rows (0 to 63, 64 to 127, ...) at most 36 rows name the same one
- gates: float32 [2048, 8], P(('expert', 'tok')), may hold values from 0.05 to 1
- upstream: bfloat16 [2048, 3584], P(('expert', 'tok')), may hold values from -6 to 6
- w_up: bfloat16 [16, 3584, 1024], P('expert', None, 'tok'), may hold values from -0.09375 to 0.09375
- w_down: bfloat16 [16, 1024, 3584], P('expert', 'tok'), may hold values from -0.1875 to 0.1875
Outputs:
- mixed: bfloat16 [2048, 3584], P(('expert', 'tok'))
- d_tokens: bfloat16 [2048, 3584], P(('expert', 'tok'))
- d_gates: float32 [2048, 8], P(('expert', 'tok'))
- grad_up: bfloat16 [16, 3584, 1024], P('expert', None, 'tok')
- grad_down: bfloat16 [16, 1024, 3584], P('expert', 'tok')
Inputs may be any that keep to these rules, and one draw needn't show every extreme that they name: `routes`: each token names 8 different experts. At most 36 of the 64 tokens of one device name the same expert, and in every draw the tokens of some device name some expert exactly 36 times.
All inputs are finite; a program needn't handle non-finite values.
Results may differ from a plain program's by a relative error of at most 0.0065.
Values may be sent and summed in bfloat16 or wider, within the bound.
A program may use at most 192 MiB of HBM per device.

v0:
```python
import jax
import jax.numpy as jnp
from jax import lax
from jax.sharding import PartitionSpec as P

GELU_C = 0.7978845608028654
GELU_A = 0.044715


def gelu_value(hidden):
    inner_arg = GELU_C * (hidden + GELU_A * hidden * hidden * hidden)
    return 0.5 * hidden * (1.0 + jnp.tanh(inner_arg))


def gelu_slope(hidden):
    tangent = jnp.tanh(GELU_C * (hidden + GELU_A * hidden * hidden * hidden))
    return 0.5 * (1.0 + tangent) + 0.5 * hidden * (1.0 - tangent * tangent) * GELU_C * (
        1.0 + 3.0 * GELU_A * hidden * hidden
    )


def expert_rows(rows_x, rows_grad, up_local, down_local):
    hidden = jnp.dot(rows_x, up_local, preferred_element_type=jnp.float32)
    active = gelu_value(hidden).astype(jnp.bfloat16)
    out_part = jnp.dot(active, down_local, preferred_element_type=jnp.float32)
    d_active = lax.dot_general(
        rows_grad, down_local, (((1,), (1,)), ((), ())), preferred_element_type=jnp.float32
    )
    d_hidden = (d_active * gelu_slope(hidden)).astype(jnp.bfloat16)
    dx_part = lax.dot_general(
        d_hidden, up_local, (((1,), (1,)), ((), ())), preferred_element_type=jnp.float32
    )
    grad_down = lax.dot_general(
        active, rows_grad, (((0,), (0,)), ((), ())), preferred_element_type=jnp.float32
    )
    grad_up = lax.dot_general(
        rows_x, d_hidden, (((0,), (0,)), ((), ())), preferred_element_type=jnp.float32
    )
    return (out_part, dx_part, grad_up, grad_down)


def shards(tokens, routes, gates, upstream, w_up, w_down):
    tok_rows, feature_width = tokens.shape
    top_count = routes.shape[1]
    owners = lax.axis_size("expert")
    pair_count = lax.axis_size("tok")
    capacity = tok_rows * top_count // owners + max(1, tok_rows * top_count // (8 * owners))
    assigned = routes.reshape(-1)
    labels = jnp.arange(owners, dtype=jnp.int32)
    onehot = (assigned[:, None] == labels[None, :]).astype(jnp.int32)
    earlier = jnp.cumsum(onehot, axis=0) - onehot
    slot_rank = jnp.sum(earlier * onehot, axis=1)
    slot_of = assigned * capacity + slot_rank
    slot_ids = jnp.arange(owners * capacity, dtype=jnp.int32)
    matches = (slot_of[None, :] == slot_ids[:, None]).astype(jnp.int32)
    filled = jnp.sum(matches, axis=1) > 0
    source = jnp.sum(matches * jnp.arange(assigned.shape[0], dtype=jnp.int32)[None, :], axis=1)
    token_ids = source // top_count
    send_x = jnp.where(filled[:, None], tokens[token_ids], jnp.zeros((), jnp.bfloat16))
    gate_rows = jnp.where(filled, gates.reshape(-1)[source], jnp.zeros((), jnp.float32))
    send_grad = (gate_rows[:, None] * upstream[token_ids].astype(jnp.float32)).astype(jnp.bfloat16)
    send_x = send_x.reshape(owners, capacity, feature_width)
    send_grad = send_grad.reshape(owners, capacity, feature_width)
    recv_x, recv_grad = (
        lax.all_to_all(send_x, "expert", split_axis=0, concat_axis=0, tiled=True),
        lax.all_to_all(send_grad, "expert", split_axis=0, concat_axis=0, tiled=True),
    )
    both_x, both_grad = (
        lax.all_gather(recv_x[None], "tok", axis=0, tiled=True),
        lax.all_gather(recv_grad[None], "tok", axis=0, tiled=True),
    )
    rows_x = both_x.reshape(-1, feature_width)
    rows_grad = both_grad.reshape(-1, feature_width)
    out_part, dx_part, grad_up, grad_down = expert_rows(rows_x, rows_grad, w_up[0], w_down[0])
    shaped_out = out_part.reshape(pair_count, owners, capacity, feature_width)
    shaped_dx = dx_part.reshape(pair_count, owners, capacity, feature_width)
    summed_out, summed_dx = (
        lax.psum_scatter(shaped_out, "tok", scatter_dimension=0, tiled=True),
        lax.psum_scatter(shaped_dx, "tok", scatter_dimension=0, tiled=True),
    )
    home_out, home_dx = (
        lax.all_to_all(
            summed_out[0].astype(jnp.bfloat16), "expert", split_axis=0, concat_axis=0, tiled=True
        ),
        lax.all_to_all(
            summed_dx[0].astype(jnp.bfloat16), "expert", split_axis=0, concat_axis=0, tiled=True
        ),
    )
    out_pairs = (
        home_out.reshape(owners * capacity, feature_width)[slot_of]
        .reshape(tok_rows, top_count, feature_width)
        .astype(jnp.float32)
    )
    dx_pairs = (
        home_dx.reshape(owners * capacity, feature_width)[slot_of]
        .reshape(tok_rows, top_count, feature_width)
        .astype(jnp.float32)
    )
    mixed_out = jnp.sum(gates[:, :, None] * out_pairs, axis=1).astype(jnp.bfloat16)
    d_gates = jnp.sum(upstream.astype(jnp.float32)[:, None, :] * out_pairs, axis=2)
    d_tokens = jnp.sum(dx_pairs, axis=1).astype(jnp.bfloat16)
    return (
        mixed_out,
        d_tokens,
        d_gates,
        grad_up.astype(jnp.bfloat16)[None],
        grad_down.astype(jnp.bfloat16)[None],
    )


def solution(mesh):
    return jax.shard_map(
        shards,
        mesh=mesh,
        in_specs=(
            P(("expert", "tok"), None),
            P(("expert", "tok"), None),
            P(("expert", "tok"), None),
            P(("expert", "tok"), None),
            P("expert", None, "tok"),
            P("expert", "tok", None),
        ),
        out_specs=(
            P(("expert", "tok"), None),
            P(("expert", "tok"), None),
            P(("expert", "tok"), None),
            P("expert", None, "tok"),
            P("expert", "tok", None),
        ),
        check_vma=False,
    )
```

profile of v0, /device:TPU:14, one launch (start us, length us, event | category | flops | bytes accessed | tf_op | source)
XLA Modules:
  0.0 616.5 jit_solution(9409691657999771369)
XLA Ops:
  7.2 0.8 copy.30
  8.0 0.1 reshape.202
  8.2 1.2 reduce-window.6
  9.4 0.2 slice_reduce_fusion
  9.6 0.1 fusion.25
  9.7 0.4 convert_reduce_fusion
  10.1 0.1 gt.14
  10.3 5.0 gather_fusion
  15.3 6.9 %gather.20 = bf16[16,36,3584]{2,1,0:T(8,128)(2,1)} reshape(bf16[576,3584]{1,0:T(8,128)(2,1)} %gather_fusion) | data formatting | bytes 8257536 | tf_op jit(solution)/shard_map/gather | solution.py:59
  22.2 4.7 broadcast_select_fusion
  26.9 7.3 %all-to-all-start = ((bf16[16,36,3584]{2,1,0:T(8,128)(2,1)}), bf16[16,36,3584]{2,1,0:T(8,128)(2,1)}, u32[]{:S(2)}, u32[]{:S(2)}) async-start(bf16[16,36,3584]{2,1,0:T(8,128)(2,1)} %broadcast_select_fusion), calls=%async_computation | async-start | bytes 9175040 | tf_op jit(solution)/shard_map/all_to_all | solution.py:65
  34.4 4.0 gather_fusion.2
  38.5 4.9 gather_fusion.3
  43.4 7.6 %reshape.211 = f32[16,36,3584]{2,1,0:T(8,128)} reshape(bf16[576,3584]{1,0:T(8,128)(2,1)} %gather_fusion.3) | data formatting | bytes 12386304 | tf_op jit(solution)/shard_map/convert_element_type | solution.py:61
  51.0 86.7 %all-to-all-done = bf16[16,36,3584]{2,1,0:T(8,128)(2,1)} async-done(((bf16[16,36,3584]{2,1,0:T(8,128)(2,1)}), bf16[16,36,3584]{2,1,0:T(8,128)(2,1)}, u32[]{:S(2)}, u32[]{:S(2)}) %all-to-all-start) | async-done | bytes 4128800 | tf_op jit(solution)/shard_map/all_to_all | solution.py:65
  137.7 5.4 copy.33
  143.3 4.9 multiply_convert_fusion
  148.1 104.5 %all_to_all.20 = bf16[16,36,3584]{2,1,0:T(8,128)(2,1)S(1)} all-to-all(bf16[16,36,3584]{2,1,0:T(8,128)(2,1)S(1)} %multiply_convert_fusion), channel_id=1, replica_groups=mesh['expert'=16,'tok'=2] {'expert'}, dimensions={0} | all-to-all | bytes 8257536 | tf_op jit(solution)/shard_map/all_to_all | solution.py:66
  252.6 3.2 copy.37
  255.8 0.2 reduce-scatter.5.cloned.1.call-start
  256.1 12.7 %copy.34 = bf16[32,36,3584]{2,1,0:T(8,128)(2,1)} copy(bf16[32,36,3584]{2,0,1:T(8,128)(2,1)} %all-gather.5.cloned.1.call-done) | data formatting | bytes 16515072 | tf_op jit(solution)/shard_map/all_gather | solution.py:69
  268.8 12.7 %reshape.204 = bf16[1152,3584]{1,0:T(8,128)(2,1)} reshape(bf16[32,36,3584]{2,1,0:T(8,128)(2,1)} %copy.34) | data formatting | bytes 16515072 | tf_op jit(solution)/shard_map/reshape | solution.py:72
  281.5 11.4 %copy.38 = bf16[32,36,3584]{2,1,0:T(8,128)(2,1)} copy(bf16[32,36,3584]{2,0,1:T(8,128)(2,1)} %all-gather.7.cloned.1.call-done) | data formatting | bytes 16515072 | tf_op jit(solution)/shard_map/all_gather | solution.py:70
  292.9 12.6 %reshape.207 = bf16[1152,3584]{1,0:T(8,128)(2,1)} reshape(bf16[32,36,3584]{2,1,0:T(8,128)(2,1)} %copy.38) | data formatting | bytes 16515072 | tf_op jit(solution)/shard_map/reshape | solution.py:73
  305.5 10.6 %multiply_convert_fusion.1 = (bf16[1152,512]{1,0:T(8,128)(2,1)}, f32[1152,512]{1,0:T(8,128)S(1)}) fusion(bf16[1152,3584]{1,0:T(8,128)(2,1)} %reshape.204, bf16[1,3584,512]{2,1,0:T(8,128)(2,1)} %param.10), kind=kOutput, calls=%fused_computation.35 | convolution fusion | flops 4233166848 | bytes 15466496 | tf_op jit(solution)/shard_map/dot_general | solution.py:23
  316.1 5.8 fusion.15
  321.9 0.7 dot_general.26
  322.6 10.9 %fusion.4 = f32[2,16,36,3584]{3,2,1,0:T(8,128)} fusion(bf16[2,16,36,512]{3,2,1,0:T(8,128)(2,1)S(1)} %dot_general.26, bf16[1,3584,512]{2,1,0:T(8,128)(2,1)} %param.10), kind=kOutput, calls=%fused_computation.17 | convolution fusion | flops 4227858432 | bytes 21364736 | tf_op jit(solution)/shard_map/dot_general | solution.py:30
  333.6 2.1 dot_general.23
  335.7 14.5 %fusion.6 = f32[2,16,36,3584]{3,2,1,0:T(8,128)} fusion(bf16[2,16,36,512]{3,2,1,0:T(8,128)(2,1)S(1)} %dot_general.23, bf16[1,512,3584]{2,1,0:T(8,128)(2,1)} %param.11), kind=kOutput, calls=%fused_computation.19 | convolution fusion | flops 4227858432 | bytes 21364736 | tf_op jit(solution)/shard_map/dot_general | solution.py:25
  350.2 11.6 %reduce-scatter.5.cloned.1.call-done = f32[1,16,36,3584]{3,2,1,0:T(8,128)} async-done(((f32[2,16,36,3584]{3,2,1,0:T(8,128)}), f32[1,16,36,3584]{3,2,1,0:T(8,128)}) %reduce-scatter.5.cloned.1.call-update) | async-done | bytes 8257552 | tf_op jit(solution)/shard_map/reduce_scatter | solution.py:79
  361.8 6.3 %convert_bitcast_fusion = bf16[16,36,3584]{2,1,0:T(8,128)(2,1)} fusion(f32[1,16,36,3584]{3,2,1,0:T(8,128)} %reduce-scatter.5.cloned.1.call-done), kind=kLoop, calls=%fused_computation.14 | loop fusion | flops 2064384 | bytes 12386304 | tf_op jit(solution)/shard_map/convert_element_type | solution.py:86
  368.1 7.0 %all-to-all-start.3 = ((bf16[16,36,3584]{2,1,0:T(8,128)(2,1)}), bf16[16,36,3584]{2,1,0:T(8,128)(2,1)}, u32[]{:S(2)}, u32[]{:S(2)}) async-start(bf16[16,36,3584]{2,1,0:T(8,128)(2,1)} %convert_bitcast_fusion), calls=%async_computation.5 | async-start | bytes 9175040 | tf_op jit(solution)/shard_map/all_to_all | solution.py:85
  375.0 18.0 %reduce-scatter.3.cloned.1.call-done = f32[1,16,36,3584]{3,2,1,0:T(8,128)} async-done(((f32[2,16,36,3584]{3,2,1,0:T(8,128)}), f32[1,16,36,3584]{3,2,1,0:T(8,128)}) %reduce-scatter.3.cloned.1.call-update) | async-done | bytes 8257552 | tf_op jit(solution)/shard_map/reduce_scatter | solution.py:78
  393.0 6.2 %convert_bitcast_fusion.1 = bf16[16,36,3584]{2,1,0:T(8,128)(2,1)} fusion(f32[1,16,36,3584]{3,2,1,0:T(8,128)} %reduce-scatter.3.cloned.1.call-done), kind=kLoop, calls=%fused_computation.15 | loop fusion | flops 2064384 | bytes 12386304 | tf_op jit(solution)/shard_map/convert_element_type | solution.py:83
  399.2 80.1 %all-to-all-done.3 = bf16[16,36,3584]{2,1,0:T(8,128)(2,1)} async-done(((bf16[16,36,3584]{2,1,0:T(8,128)(2,1)}), bf16[16,36,3584]{2,1,0:T(8,128)(2,1)}, u32[]{:S(2)}, u32[]{:S(2)}) %all-to-all-start.3) | async-done | bytes 4128800 | tf_op jit(solution)/shard_map/all_to_all | solution.py:85
  479.2 5.4 all-to-all-start.1
  484.8 0.1 mul.128
  484.9 10.5 %fusion.3 = bf16[1,512,3584]{2,1,0:T(8,128)(2,1)} fusion(bf16[1152,512]{1,0:T(8,128)(2,1)} %get-tuple-element.21, bf16[1152,3584]{1,0:T(8,128)(2,1)} %reshape.207), kind=kOutput, calls=%fused_computation.13 | convolution fusion | flops 4229693440 | bytes 13107200 | tf_op jit(solution)/shard_map/dot_general | solution.py:33
  495.4 9.8 %fusion.2 = bf16[1,3584,512]{2,1,0:T(8,128)(2,1)} fusion(bf16[1152,3584]{1,0:T(8,128)(2,1)} %reshape.204, bf16[1152,512]{1,0:T(8,128)(2,1)S(1)} %fusion.15), kind=kOutput, calls=%fused_computation.12 | convolution fusion | flops 4229693440 | bytes 13107200 | tf_op jit(solution)/shard_map/dot_general | solution.py:36
  505.2 6.9 %reshape.208 = bf16[576,3584]{1,0:T(8,128)(2,1)} reshape(bf16[16,36,3584]{2,1,0:T(8,128)(2,1)} %all-to-all-done.3) | data formatting | bytes 8257536 | tf_op jit(solution)/shard_map/reshape | solution.py:95
  512.1 10.7 %gather_fusion.4 = bf16[512,3584]{1,0:T(8,128)(2,1)} fusion(bf16[576,3584]{1,0:T(8,128)(2,1)} %reshape.208, s32[1024]{0:T(1024)S(1)} %pad_clamp_fusion.1), kind=kCustom, calls=%fused_computation.4 | custom fusion | bytes 7342080 | tf_op jit(solution)/shard_map/gather | solution.py:95
  522.9 5.3 bitcast_reduce_fusion
  528.2 57.7 %all-to-all-done.1 = bf16[16,36,3584]{2,1,0:T(8,128)(2,1)} async-done(((bf16[16,36,3584]{2,1,0:T(8,128)(2,1)}), bf16[16,36,3584]{2,1,0:T(8,128)(2,1)}, u32[]{:S(2)}, u32[]{:S(2)}) %all-to-all-start.1) | async-done | bytes 4128800 | tf_op jit(solution)/shard_map/all_to_all | solution.py:82
  585.9 6.9 %reshape.205 = bf16[576,3584]{1,0:T(8,128)(2,1)} reshape(bf16[16,36,3584]{2,1,0:T(8,128)(2,1)} %all-to-all-done.1) | data formatting | bytes 8257536 | tf_op jit(solution)/shard_map/reshape | solution.py:90
  592.8 10.7 %gather_fusion.1 = bf16[512,3584]{1,0:T(8,128)(2,1)} fusion(bf16[576,3584]{1,0:T(8,128)(2,1)} %reshape.205, s32[1024]{0:T(1024)S(1)} %pad_clamp_fusion.1), kind=kCustom, calls=%fused_computation.1 | custom fusion | bytes 7342080 | tf_op jit(solution)/shard_map/gather | solution.py:90
  603.5 5.6 fusion.1
  609.1 0.7 copy.39
  (44 shorter events, 0.9 us)
Async XLA Ops:
  7.2 3.1 copy-start
  26.9 7.3 %copy-start.7 = (f32[64,8]{0,1:T(8,128)S(1)}, f32[64,8]{0,1:T(8,128)}, u32[]{:S(2)}) copy-start(f32[64,8]{0,1:T(8,128)} %param.8) | copy-start | bytes 6148
  26.9 110.8 %all-to-all-start = ((bf16[16,36,3584]{2,1,0:T(8,128)(2,1)}), bf16[16,36,3584]{2,1,0:T(8,128)(2,1)}, u32[]{:S(2)}, u32[]{:S(2)}) async-start(bf16[16,36,3584]{2,1,0:T(8,128)(2,1)} %broadcast_select_fusion), calls=%async_computation | async-start | bytes 9175040 | tf_op jit(solution)/shard_map/all_to_all | solution.py:65
  34.2 4.3 copy-start.2
  34.2 221.9 %all-gather.5.cloned.1.call-start = ((), (), s32[]{:S(2)}) async-start(), calls=%async_computation.8 | async-start | bytes 12386304 | tf_op jit(solution)/shard_map/all_gather | solution.py:69
  34.3 9.1 %copy-start.4 = (f32[64,8]{1,0:T(8,128)}, f32[64,8]{1,0:T(8,128)S(1)}, u32[]{:S(2)}) copy-start(f32[64,8]{1,0:T(8,128)S(1)} %copy.29) | copy-start | bytes 6148
  143.2 138.3 %all-gather.7.cloned.1.call-start = ((), (), s32[]{:S(2)}) async-start(), calls=%async_computation.9 | async-start | bytes 12386304 | tf_op jit(solution)/shard_map/all_gather | solution.py:70
  255.8 106.0 %reduce-scatter.5.cloned.1.call-start = ((), (), s32[]{:S(2)}) async-start(), calls=%async_computation.7 | async-start | bytes 27525120 | tf_op jit(solution)/shard_map/reduce_scatter | solution.py:79
  305.5 10.6 %copy-start.3 = (bf16[1152,3584]{1,0:T(8,128)(2,1)S(1)}, bf16[1152,3584]{1,0:T(8,128)(2,1)}, u32[]{:S(2)}) copy-start(bf16[1152,3584]{1,0:T(8,128)(2,1)} %reshape.207) | copy-start | bytes 24772612
  305.5 10.6 %copy-start.8 = (bf16[1,512,3584]{2,1,0:T(8,128)(2,1)S(1)}, bf16[1,512,3584]{2,1,0:T(8,128)(2,1)}, u32[]{:S(2)}) copy-start(bf16[1,512,3584]{2,1,0:T(8,128)(2,1)} %param.11) | copy-start | bytes 11010052
  333.5 59.5 %reduce-scatter.3.cloned.1.call-start = ((), (), s32[]{:S(2)}) async-start(), calls=%async_computation.6 | async-start | bytes 27525120 | tf_op jit(solution)/shard_map/reduce_scatter | solution.py:78
  368.1 111.1 %all-to-all-start.3 = ((bf16[16,36,3584]{2,1,0:T(8,128)(2,1)}), bf16[16,36,3584]{2,1,0:T(8,128)(2,1)}, u32[]{:S(2)}, u32[]{:S(2)}) async-start(bf16[16,36,3584]{2,1,0:T(8,128)(2,1)} %convert_bitcast_fusion), calls=%async_computation.5 | async-start | bytes 9175040 | tf_op jit(solution)/shard_map/all_to_all | solution.py:85
  399.2 85.5 %copy-start.6 = (s32[64,8]{0,1:T(8,128)S(1)}, s32[64,8]{0,1:T(8,128)}, u32[]{:S(2)}) copy-start(s32[64,8]{0,1:T(8,128)} %param.7) | copy-start | bytes 6148
  479.2 106.7 %all-to-all-start.1 = ((bf16[16,36,3584]{2,1,0:T(8,128)(2,1)}), bf16[16,36,3584]{2,1,0:T(8,128)(2,1)}, u32[]{:S(2)}, u32[]{:S(2)}) async-start(bf16[16,36,3584]{2,1,0:T(8,128)(2,1)} %convert_bitcast_fusion.1), calls=%async_computation.2 | async-start | bytes 9175040 | tf_op jit(solution)/shard_map/all_to_all | solution.py:82
  592.8 10.7 %copy-start.5 = (f32[64,8]{1,0:T(8,128)S(1)}, f32[64,8]{1,0:T(8,128)}, u32[]{:S(2)}) copy-start(f32[64,8]{1,0:T(8,128)} %copy-done.4) | copy-start | bytes 6148
  592.8 16.9 %copy-start.1 = (bf16[64,3584]{1,0:T(8,128)(2,1)S(1)}, bf16[64,3584]{1,0:T(8,128)(2,1)}, u32[]{:S(2)}) copy-start(bf16[64,3584]{1,0:T(8,128)(2,1)} %param.6) | copy-start | bytes 1376260
Sparse Core Ops, SparseCore 0:
  143.3 18.9 all-gather.4
  256.0 19.9 all-gather.6
  333.6 28.1 reduce-scatter.4
  364.0 28.9 reduce-scatter.2
where the time goes:
time: 625 us; the launch traced here: 616 us
  waiting for transfers between devices  254 us (41%)
  local copies, waits for them, and re-layouts  127 us (20%)
  blocking collectives  105 us (17%)
  matrix products  62.1 us (10%)
  other arithmetic  34.7 us (6%)
  starting transfers between devices  20 us (3%)
  between operations  14.2 us (2%)
    all_to_all x1, blocking collectives, shards(): lax.all_to_all(send_grad, 'expert', split_axis=0, concat_axis=0, tiled=True)  105 us
    all_to_all x1, waiting for transfers between devices, shards(): lax.all_to_all(send_x, 'expert', split_axis=0, concat_axis=0, tiled=True)  86.7 us
    all_to_all x1, waiting for transfers between devices, shards(): lax.all_to_all(summed_dx[0].astype(jnp.bfloat16), 'expert', split_axis=0,...  80.1 us
    all_to_all x1, waiting for transfers between devices, shards(): lax.all_to_all(summed_out[0].astype(jnp.bfloat16), 'expert', split_axis=0...  57.7 us
    reduce_scatter x1, waiting for transfers between devices, shards(): lax.psum_scatter(shaped_out, 'tok', scatter_dimension=0, tiled=True)  18 us
    dot_general x1, matrix products, expert_rows(): out_part = jnp.dot(active, down_local, preferred_element_type=jnp.float32)  14.5 us
    all_gather x1, local copies, waits for them, and re-layouts, shards(): lax.all_gather(recv_x[None], 'tok', axis=0, tiled=True)  12.7 us
    reshape x1, local copies, waits for them, and re-layouts, shards(): rows_x = both_x.reshape(-1, feature_width)  12.7 us
  transfers between devices with their start and end apart: 7, of which 5 were waited for; matrix products, arithmetic and copies ran while one was open for 20% of the time, Pallas kernels for 0%

commit v1 on v0

--- a/solution.py
+++ b/solution.py
@@ -40,6 +40,25 @@
 
 
 def shards(tokens, routes, gates, upstream, w_up, w_down):
+
+    def apply_slots(mat):
+        view_out, d_next = (jax.lax.axis_size("expert"), jax.lax.axis_index("expert"))
+        local_part = mat.shape[0] // view_out
+        block_next = jnp.roll(mat, -d_next * local_part, axis=0)
+        stack_in = [lax.slice_in_dim(block_next, 0, local_part, axis=0)]
+        for pp in range(1, view_out):
+            response = lax.slice_in_dim(block_next, pp * local_part, (pp + 1) * local_part, axis=0)
+            stack_in.append(
+                jax.lax.ppermute(
+                    response,
+                    axis_name="expert",
+                    perm=[(c, (c + pp) % view_out) for c in range(view_out)],
+                )
+            )
+        return jnp.roll(
+            jnp.concatenate(stack_in[::-1], 0), (d_next + 1) * stack_in[0].shape[0], axis=0
+        )
+
     tok_rows, feature_width = tokens.shape
     top_count = routes.shape[1]
     owners = lax.axis_size("expert")
@@ -62,7 +81,7 @@
     send_x = send_x.reshape(owners, capacity, feature_width)
     send_grad = send_grad.reshape(owners, capacity, feature_width)
     recv_x, recv_grad = (
-        lax.all_to_all(send_x, "expert", split_axis=0, concat_axis=0, tiled=True),
+        apply_slots(send_x),
         lax.all_to_all(send_grad, "expert", split_axis=0, concat_axis=0, tiled=True),
     )
     both_x, both_grad = (

time: 625 us -> 663 us (1.061)
  starting transfers between devices: 20 us -> 74.5 us
  waiting for transfers between devices: 254 us -> 225 us
    all_to_all x1 -> x0, waiting for transfers between devices: 86.7 us -> none  [shards(): lax.all_to_all(send_x, 'expert', split_axis=0, concat_axis=0, tiled=True)]
    ppermute x0 -> x15, waiting for transfers between devices: none -> 72.6 us  [apply_slots(): jax.lax.ppermute(response, axis_name='expert', perm=[(c, (c + pp) % view_...]
    ppermute x0 -> x15, starting transfers between devices: none -> 61.7 us  [apply_slots(): jax.lax.ppermute(response, axis_name='expert', perm=[(c, (c + pp) % view_...]
    all_to_all x1, waiting for transfers between devices: 80.1 us -> 57.6 us  [shards(): lax.all_to_all(summed_dx[0].astype(jnp.bfloat16), 'expert', split_axis=0,...]
    all_to_all x1, waiting for transfers between devices: 57.7 us -> 79.2 us  [shards(): lax.all_to_all(summed_out[0].astype(jnp.bfloat16), 'expert', split_axis=0...]
    reduce_scatter x1, waiting for transfers between devices: 18 us -> 0.02 us  [shards(): lax.psum_scatter(shaped_out, 'tok', scatter_dimension=0, tiled=True)]
    all_to_all x1 -> x0, starting transfers between devices: 7.27 us -> none  [shards(): lax.all_to_all(send_x, 'expert', split_axis=0, concat_axis=0, tiled=True)]
  transfers between devices with their start and end apart: 7 -> 21, of which waited for: 5 -> 13; matrix products, arithmetic and copies ran while one was open for 20% -> 28% of each run, Pallas kernels for 0% -> 0%
where the time goes in v1:
time: 663 us; the launch traced here: 655 us
  waiting for transfers between devices  225 us (34%)
  local copies, waits for them, and re-layouts  133 us (20%)
  blocking collectives  107 us (16%)
  starting transfers between devices  74.5 us (11%)
  matrix products  64.1 us (10%)
  other arithmetic  36.2 us (5%)
  between operations  14.6 us (2%)
    all_to_all x1, blocking collectives, shards(): lax.all_to_all(send_grad, 'expert', split_axis=0, concat_axis=0, tiled=True)  107 us
    all_to_all x1, waiting for transfers between devices, shards(): lax.all_to_all(summed_out[0].astype(jnp.bfloat16), 'expert', split_axis=0...  79.2 us
    ppermute x15, waiting for transfers between devices, apply_slots(): jax.lax.ppermute(response, axis_name='expert', perm=[(c, (c + pp) % view_...  72.6 us
    ppermute x15, starting transfers between devices, apply_slots(): jax.lax.ppermute(response, axis_name='expert', perm=[(c, (c + pp) % view_...  61.7 us
    all_to_all x1, waiting for transfers between devices, shards(): lax.all_to_all(summed_dx[0].astype(jnp.bfloat16), 'expert', split_axis=0,...  57.6 us
    reduce_scatter x1, waiting for transfers between devices, shards(): lax.psum_scatter(shaped_dx, 'tok', scatter_dimension=0, tiled=True)  15.1 us
    reshape x1, local copies, waits for them, and re-layouts, shards(): rows_grad = both_grad.reshape(-1, feature_width)  13.8 us
    all_gather x1, local copies, waits for them, and re-layouts, shards(): lax.all_gather(recv_grad[None], 'tok', axis=0, tiled=True)  13.5 us
  transfers between devices with their start and end apart: 21, of which 13 were waited for; matrix products, arithmetic and copies ran while one was open for 28% of the time, Pallas kernels for 0%

profile of v1, /device:TPU:14, one launch (start us, length us, event | category | flops | bytes accessed | tf_op | source)
XLA Modules:
  0.0 654.8 jit_solution(5750851344823024086)
XLA Ops:
  11.0 5.0 gather_fusion
  16.0 6.9 %gather.20 = bf16[16,36,3584]{2,1,0:T(8,128)(2,1)} reshape(bf16[576,3584]{1,0:T(8,128)(2,1)} %gather_fusion) | data formatting | bytes 8257536 | tf_op jit(solution)/shard_map/gather | solution.py:78
  31.7 3.3 collective-permute-start.14
  36.5 3.4 collective-permute-start.11
  40.1 4.0 gather_fusion.2
  44.1 4.9 gather_fusion.3
  49.1 7.6 %reshape.211 = f32[16,36,3584]{2,1,0:T(8,128)} reshape(bf16[576,3584]{1,0:T(8,128)(2,1)} %gather_fusion.3) | data formatting | bytes 12386304 | tf_op jit(solution)/shard_map/convert_element_type | solution.py:80
  56.7 8.5 %collective-permute-done.1 = bf16[1,36,3584]{2,1,0:T(8,128)(2,1)S(1)} collective-permute-done((bf16[1,36,3584]{2,1,0:T(8,128)(2,1)}, bf16[1,36,3584]{2,1,0:T(8,128)(2,1)S(1)}, u32[]{:S(2)}, u32[]{:S(2)}) %collective-permute-start.1) | collective-permute-done | bytes 258080 | tf_op jit(solution)/shard_map/ppermute | solution.py:52
  66.8 6.3 collective-permute-done.2
  73.0 3.3 collective-permute-start.3
  76.3 4.4 collective-permute-done.3
  80.8 6.5 collective-permute-start.4
  87.3 4.4 collective-permute-done.4
  91.7 8.4 %collective-permute-start.5 = (bf16[1,36,3584]{2,1,0:T(8,128)(2,1)}, bf16[1,36,3584]{2,1,0:T(8,128)(2,1)S(1)}, u32[]{:S(2)}, u32[]{:S(2)}) collective-permute-start(bf16[1,36,3584]{2,1,0:T(8,128)(2,1)} %get-tuple-element.31), channel_id=1, source_target_pairs={{0,20},{2,22},{4,24},{6,26},{8,28},{10,30},{12,0},{14,2},{16,4},{1... | collective-permute-start | bytes 774152 | tf_op jit(solution)/shard_map/ppermute | solution.py:52
  100.1 6.2 collective-permute-done.5
  109.2 6.6 %collective-permute-done.6 = bf16[1,36,3584]{2,1,0:T(8,128)(2,1)S(1)} collective-permute-done((bf16[1,36,3584]{2,1,0:T(8,128)(2,1)}, bf16[1,36,3584]{2,1,0:T(8,128)(2,1)S(1)}, u32[]{:S(2)}, u32[]{:S(2)}) %collective-permute-start.6) | collective-permute-done | bytes 258080 | tf_op jit(solution)/shard_map/ppermute | solution.py:52
  115.8 27.1 %collective-permute-start.7 = (bf16[1,36,3584]{2,1,0:T(8,128)(2,1)S(1)}, bf16[1,36,3584]{2,1,0:T(8,128)(2,1)S(1)}, u32[]{:S(2)}, u32[]{:S(2)}) collective-permute-start(bf16[1,36,3584]{2,1,0:T(8,128)(2,1)S(1)} %get-tuple-element.29), channel_id=1, source_target_pairs={{0,16},{2,18},{4,20},{6,22},{8,24},{10,26},{12,28},{14,30},{16,0},... | collective-permute-start | bytes 774152 | tf_op jit(solution)/shard_map/ppermute | solution.py:52
  142.9 5.9 collective-permute-done.7
  148.8 13.5 %collective-permute-done.8 = bf16[1,36,3584]{2,1,0:T(8,128)(2,1)S(1)} collective-permute-done((bf16[1,36,3584]{2,1,0:T(8,128)(2,1)}, bf16[1,36,3584]{2,1,0:T(8,128)(2,1)S(1)}, u32[]{:S(2)}, u32[]{:S(2)}) %collective-permute-start.8) | collective-permute-done | bytes 258080 | tf_op jit(solution)/shard_map/ppermute | solution.py:52
  162.3 7.5 %collective-permute-done.9 = bf16[1,36,3584]{2,1,0:T(8,128)(2,1)S(1)} collective-permute-done((bf16[1,36,3584]{2,1,0:T(8,128)(2,1)S(1)}, bf16[1,36,3584]{2,1,0:T(8,128)(2,1)S(1)}, u32[]{:S(2)}, u32[]{:S(2)}) %collective-permute-start.9) | collective-permute-done | bytes 258080 | tf_op jit(solution)/shard_map/ppermute | solution.py:52
  169.9 3.4 collective-permute-start.10
  173.3 9.2 %collective-permute-done.10 = bf16[1,36,3584]{2,1,0:T(8,128)(2,1)S(1)} collective-permute-done((bf16[1,36,3584]{2,1,0:T(8,128)(2,1)S(1)}, bf16[1,36,3584]{2,1,0:T(8,128)(2,1)S(1)}, u32[]{:S(2)}, u32[]{:S(2)}) %collective-permute-start.10) | collective-permute-done | bytes 258080 | tf_op jit(solution)/shard_map/ppermute | solution.py:52
  185.4 3.2 copy.33
  188.7 4.9 multiply_convert_fusion
  193.6 107.3 %all_to_all.15 = bf16[16,36,3584]{2,1,0:T(8,128)(2,1)S(1)} all-to-all(bf16[16,36,3584]{2,1,0:T(8,128)(2,1)S(1)} %multiply_convert_fusion), channel_id=1, replica_groups=mesh['expert'=16,'tok'=2] {'expert'}, dimensions={0} | all-to-all | bytes 8257536 | tf_op jit(solution)/shard_map/all_to_all | solution.py:85
  304.7 12.7 %copy.34 = bf16[32,36,3584]{2,1,0:T(8,128)(2,1)} copy(bf16[32,36,3584]{2,0,1:T(8,128)(2,1)} %all-gather.5.cloned.1.call-done) | data formatting | bytes 16515072 | tf_op jit(solution)/shard_map/all_gather | solution.py:88
  317.4 12.7 %reshape.204 = bf16[1152,3584]{1,0:T(8,128)(2,1)} reshape(bf16[32,36,3584]{2,1,0:T(8,128)(2,1)} %copy.34) | data formatting | bytes 16515072 | tf_op jit(solution)/shard_map/reshape | solution.py:91
  330.1 10.8 %multiply_convert_fusion.1 = (bf16[1152,512]{1,0:T(8,128)(2,1)S(1)}, f32[1152,512]{1,0:T(8,128)}) fusion(bf16[1152,3584]{1,0:T(8,128)(2,1)} %reshape.204, bf16[1,3584,512]{2,1,0:T(8,128)(2,1)} %param.12), kind=kOutput, calls=%fused_computation.41 | convolution fusion | flops 4233166848 | bytes 15466496 | tf_op jit(solution)/shard_map/dot_general | solution.py:23
  341.1 10.9 %fusion.8 = f32[2,16,36,3584]{3,2,1,0:T(8,128)} fusion(bf16[2,16,36,512]{3,2,1,0:T(8,128)(2,1)S(1)} %dot_general.23, bf16[1,512,3584]{2,1,0:T(8,128)(2,1)} %param.13), kind=kOutput, calls=%fused_computation.25 | convolution fusion | flops 4227858432 | bytes 21364736 | tf_op jit(solution)/shard_map/dot_general | solution.py:25
  352.3 13.5 %copy.38 = bf16[32,36,3584]{2,1,0:T(8,128)(2,1)} copy(bf16[32,36,3584]{2,0,1:T(8,128)(2,1)} %all-gather.7.cloned.1.call-done) | data formatting | bytes 16515072 | tf_op jit(solution)/shard_map/all_gather | solution.py:89
  365.8 13.8 %reshape.207 = bf16[1152,3584]{1,0:T(8,128)(2,1)} reshape(bf16[32,36,3584]{2,1,0:T(8,128)(2,1)} %copy.38) | data formatting | bytes 16515072 | tf_op jit(solution)/shard_map/reshape | solution.py:92
  379.6 11.9 %fusion.17 = bf16[1152,512]{1,0:T(8,128)(2,1)} fusion(bf16[1152,3584]{1,0:T(8,128)(2,1)} %reshape.207, bf16[1,512,3584]{2,1,0:T(8,128)(2,1)} %param.13, f32[1152,512]{1,0:T(8,128)} %get-tuple-element.38), kind=kOutput, calls=%fused_computation.35 | convolution fusion | flops 4239065088 | bytes 15466496 | tf_op jit(solution)/shard_map/dot_general | solution.py:26
  393.6 10.9 %fusion.6 = f32[2,16,36,3584]{3,2,1,0:T(8,128)} fusion(bf16[2,16,36,512]{3,2,1,0:T(8,128)(2,1)S(1)} %dot_general.26, bf16[1,3584,512]{2,1,0:T(8,128)(2,1)} %param.12), kind=kOutput, calls=%fused_computation.23 | convolution fusion | flops 4227858432 | bytes 21364736 | tf_op jit(solution)/shard_map/dot_general | solution.py:30
  404.6 6.2 convert_bitcast_fusion.1
  410.8 6.9 %all-to-all-start = ((bf16[16,36,3584]{2,1,0:T(8,128)(2,1)}), bf16[16,36,3584]{2,1,0:T(8,128)(2,1)}, u32[]{:S(2)}, u32[]{:S(2)}) async-start(bf16[16,36,3584]{2,1,0:T(8,128)(2,1)} %convert_bitcast_fusion.1), calls=%async_computation.1 | async-start | bytes 9175040 | tf_op jit(solution)/shard_map/all_to_all | solution.py:101
  417.7 15.1 %reduce-scatter.5.cloned.1.call-done = f32[1,16,36,3584]{3,2,1,0:T(8,128)} async-done(((f32[2,16,36,3584]{3,2,1,0:T(8,128)}), f32[1,16,36,3584]{3,2,1,0:T(8,128)}) %reduce-scatter.5.cloned.1.call-update) | async-done | bytes 8257552 | tf_op jit(solution)/shard_map/reduce_scatter | solution.py:98
  432.8 6.2 convert_bitcast_fusion
  439.0 79.2 %all-to-all-done = bf16[16,36,3584]{2,1,0:T(8,128)(2,1)} async-done(((bf16[16,36,3584]{2,1,0:T(8,128)(2,1)}), bf16[16,36,3584]{2,1,0:T(8,128)(2,1)}, u32[]{:S(2)}, u32[]{:S(2)}) %all-to-all-start) | async-done | bytes 4128800 | tf_op jit(solution)/shard_map/all_to_all | solution.py:101
  518.3 5.1 all-to-all-start.2
  523.7 9.9 %fusion.3 = bf16[1,512,3584]{2,1,0:T(8,128)(2,1)} fusion(bf16[1152,512]{1,0:T(8,128)(2,1)S(1)} %get-tuple-element.37, bf16[1152,3584]{1,0:T(8,128)(2,1)} %reshape.207), kind=kOutput, calls=%fused_computation.17 | convolution fusion | flops 4229693440 | bytes 13107200 | tf_op jit(solution)/shard_map/dot_general | solution.py:33
  533.6 9.8 %fusion.2 = bf16[1,3584,512]{2,1,0:T(8,128)(2,1)} fusion(bf16[1152,3584]{1,0:T(8,128)(2,1)} %reshape.204, bf16[1152,512]{1,0:T(8,128)(2,1)S(1)} %copy-done.4), kind=kOutput, calls=%fused_computation.16 | convolution fusion | flops 4229693440 | bytes 13107200 | tf_op jit(solution)/shard_map/dot_general | solution.py:36
  543.3 6.9 %reshape.205 = bf16[576,3584]{1,0:T(8,128)(2,1)} reshape(bf16[16,36,3584]{2,1,0:T(8,128)(2,1)} %all-to-all-done) | data formatting | bytes 8257536 | tf_op jit(solution)/shard_map/reshape | solution.py:109
  550.3 10.6 %gather_fusion.1 = bf16[512,3584]{1,0:T(8,128)(2,1)} fusion(bf16[576,3584]{1,0:T(8,128)(2,1)} %reshape.205, s32[1024]{0:T(1024)S(1)} %pad_clamp_fusion.1), kind=kCustom, calls=%fused_computation.1 | custom fusion | bytes 7342080 | tf_op jit(solution)/shard_map/gather | solution.py:109
  560.9 5.6 fusion.1
  567.2 57.6 %all-to-all-done.2 = bf16[16,36,3584]{2,1,0:T(8,128)(2,1)} async-done(((bf16[16,36,3584]{2,1,0:T(8,128)(2,1)}), bf16[16,36,3584]{2,1,0:T(8,128)(2,1)}, u32[]{:S(2)}, u32[]{:S(2)}) %all-to-all-start.2) | async-done | bytes 4128800 | tf_op jit(solution)/shard_map/all_to_all | solution.py:104
  624.7 6.9 %reshape.208 = bf16[576,3584]{1,0:T(8,128)(2,1)} reshape(bf16[16,36,3584]{2,1,0:T(8,128)(2,1)} %all-to-all-done.2) | data formatting | bytes 8257536 | tf_op jit(solution)/shard_map/reshape | solution.py:114
  631.7 10.9 %gather_fusion.4 = bf16[512,3584]{1,0:T(8,128)(2,1)} fusion(bf16[576,3584]{1,0:T(8,128)(2,1)} %reshape.208, s32[1024]{0:T(1024)S(1)} %pad_clamp_fusion.1), kind=kCustom, calls=%fused_computation.4 | custom fusion | bytes 7342080 | tf_op jit(solution)/shard_map/gather | solution.py:114
  642.6 5.3 bitcast_reduce_fusion
  (95 shorter events, 29.1 us)
Async XLA Ops:
  7.2 3.8 copy-start
  7.2 297.5 %all-gather.5.cloned.1.call-start = ((), (), s32[]{:S(2)}) async-start(), calls=%async_computation.7 | async-start | bytes 12386304 | tf_op jit(solution)/shard_map/all_gather | solution.py:88
  9.8 0.6 copy-start.7
  27.3 2.2 copy-start.3
  29.5 10.4 %copy-start.10 = (f32[64,8]{0,1:T(8,128)S(1)}, f32[64,8]{0,1:T(8,128)}, u32[]{:S(2)}) copy-start(f32[64,8]{0,1:T(8,128)} %param.10) | copy-start | bytes 6148
  29.5 14.6 %copy-start.2 = (bf16[64,3584]{1,0:T(8,128)(2,1)S(1)}, bf16[64,3584]{1,0:T(8,128)(2,1)}, u32[]{:S(2)}) copy-start(bf16[64,3584]{1,0:T(8,128)(2,1)} %param.11) | copy-start | bytes 1376260
  31.1 25.5 %collective-permute-start = (bf16[1,36,3584]{2,1,0:T(8,128)(2,1)S(1)}, bf16[1,36,3584]{2,1,0:T(8,128)(2,1)S(1)}, u32[]{:S(2)}, u32[]{:S(2)}) collective-permute-start(bf16[1,36,3584]{2,1,0:T(8,128)(2,1)S(1)} %get-tuple-element.36), channel_id=1, source_target_pairs={{0,30},{2,0},{4,2},{6,4},{8,6},{10,8},{12,10},{14,12},{16,14},{18,... | collective-permute-start | bytes 774152 | tf_op jit(solution)/shard_map/ppermute | solution.py:52
  31.7 151.0 %collective-permute-start.14 = (bf16[1,36,3584]{2,1,0:T(8,128)(2,1)S(1)}, bf16[1,36,3584]{2,1,0:T(8,128)(2,1)S(1)}, u32[]{:S(2)}, u32[]{:S(2)}) collective-permute-start(bf16[1,36,3584]{2,1,0:T(8,128)(2,1)S(1)} %get-tuple-element.22), channel_id=1, source_target_pairs={{0,2},{2,4},{4,6},{6,8},{8,10},{10,12},{12,14},{14,16},{16,18},{18... | collective-permute-start | bytes 774152 | tf_op jit(solution)/shard_map/ppermute | solution.py:52
  34.9 147.7 %collective-permute-start.13 = (bf16[1,36,3584]{2,1,0:T(8,128)(2,1)S(1)}, bf16[1,36,3584]{2,1,0:T(8,128)(2,1)S(1)}, u32[]{:S(2)}, u32[]{:S(2)}) collective-permute-start(bf16[1,36,3584]{2,1,0:T(8,128)(2,1)S(1)} %get-tuple-element.23), channel_id=1, source_target_pairs={{0,4},{2,6},{4,8},{6,10},{8,12},{10,14},{12,16},{14,18},{16,20},{1... | collective-permute-start | bytes 774152 | tf_op jit(solution)/shard_map/ppermute | solution.py:52
  35.6 147.0 %collective-permute-start.12 = (bf16[1,36,3584]{2,1,0:T(8,128)(2,1)S(1)}, bf16[1,36,3584]{2,1,0:T(8,128)(2,1)S(1)}, u32[]{:S(2)}, u32[]{:S(2)}) collective-permute-start(bf16[1,36,3584]{2,1,0:T(8,128)(2,1)S(1)} %get-tuple-element.24), channel_id=1, source_target_pairs={{0,6},{2,8},{4,10},{6,12},{8,14},{10,16},{12,18},{14,20},{16,22},{... | collective-permute-start | bytes 774152 | tf_op jit(solution)/shard_map/ppermute | solution.py:52
  36.5 146.0 %collective-permute-start.11 = (bf16[1,36,3584]{2,1,0:T(8,128)(2,1)}, bf16[1,36,3584]{2,1,0:T(8,128)(2,1)S(1)}, u32[]{:S(2)}, u32[]{:S(2)}) collective-permute-start(bf16[1,36,3584]{2,1,0:T(8,128)(2,1)} %get-tuple-element.25), channel_id=1, source_target_pairs={{0,8},{2,10},{4,12},{6,14},{8,16},{10,18},{12,20},{14,22},{16,24},... | collective-permute-start | bytes 774152 | tf_op jit(solution)/shard_map/ppermute | solution.py:52
  56.6 105.7 %copy-start.6 = (bf16[1,36,3584]{2,1,0:T(8,128)(2,1)S(1)}, bf16[1,36,3584]{2,1,0:T(8,128)(2,1)}, u32[]{:S(2)}) copy-start(bf16[1,36,3584]{2,1,0:T(8,128)(2,1)} %get-tuple-element.27) | copy-start | bytes 774148
  56.6 113.2 %copy-start.5 = (bf16[1,36,3584]{2,1,0:T(8,128)(2,1)S(1)}, bf16[1,36,3584]{2,1,0:T(8,128)(2,1)}, u32[]{:S(2)}) copy-start(bf16[1,36,3584]{2,1,0:T(8,128)(2,1)} %get-tuple-element.26) | copy-start | bytes 774148
  56.6 8.6 %collective-permute-start.1 = (bf16[1,36,3584]{2,1,0:T(8,128)(2,1)}, bf16[1,36,3584]{2,1,0:T(8,128)(2,1)S(1)}, u32[]{:S(2)}, u32[]{:S(2)}) collective-permute-start(bf16[1,36,3584]{2,1,0:T(8,128)(2,1)} %get-tuple-element.35), channel_id=1, source_target_pairs={{0,28},{2,30},{4,0},{6,2},{8,4},{10,6},{12,8},{14,10},{16,12},{18,... | collective-permute-start | bytes 774152 | tf_op jit(solution)/shard_map/ppermute | solution.py:52
  65.3 7.7 %collective-permute-start.2 = (bf16[1,36,3584]{2,1,0:T(8,128)(2,1)}, bf16[1,36,3584]{2,1,0:T(8,128)(2,1)S(1)}, u32[]{:S(2)}, u32[]{:S(2)}) collective-permute-start(bf16[1,36,3584]{2,1,0:T(8,128)(2,1)} %get-tuple-element.34), channel_id=1, source_target_pairs={{0,26},{2,28},{4,30},{6,0},{8,2},{10,4},{12,6},{14,8},{16,10},{18,... | collective-permute-start | bytes 774152 | tf_op jit(solution)/shard_map/ppermute | solution.py:52
  73.0 7.8 %collective-permute-start.3 = (bf16[1,36,3584]{2,1,0:T(8,128)(2,1)}, bf16[1,36,3584]{2,1,0:T(8,128)(2,1)S(1)}, u32[]{:S(2)}, u32[]{:S(2)}) collective-permute-start(bf16[1,36,3584]{2,1,0:T(8,128)(2,1)} %get-tuple-element.33), channel_id=1, source_target_pairs={{0,24},{2,26},{4,28},{6,30},{8,0},{10,2},{12,4},{14,6},{16,8},{18,... | collective-permute-start | bytes 774152 | tf_op jit(solution)/shard_map/ppermute | solution.py:52
  80.8 10.9 %collective-permute-start.4 = (bf16[1,36,3584]{2,1,0:T(8,128)(2,1)}, bf16[1,36,3584]{2,1,0:T(8,128)(2,1)S(1)}, u32[]{:S(2)}, u32[]{:S(2)}) collective-permute-start(bf16[1,36,3584]{2,1,0:T(8,128)(2,1)} %get-tuple-element.32), channel_id=1, source_target_pairs={{0,22},{2,24},{4,26},{6,28},{8,30},{10,0},{12,2},{14,4},{16,6},{18... | collective-permute-start | bytes 774152 | tf_op jit(solution)/shard_map/ppermute | solution.py:52
  91.7 14.6 %collective-permute-start.5 = (bf16[1,36,3584]{2,1,0:T(8,128)(2,1)}, bf16[1,36,3584]{2,1,0:T(8,128)(2,1)S(1)}, u32[]{:S(2)}, u32[]{:S(2)}) collective-permute-start(bf16[1,36,3584]{2,1,0:T(8,128)(2,1)} %get-tuple-element.31), channel_id=1, source_target_pairs={{0,20},{2,22},{4,24},{6,26},{8,28},{10,30},{12,0},{14,2},{16,4},{1... | collective-permute-start | bytes 774152 | tf_op jit(solution)/shard_map/ppermute | solution.py:52
  106.3 9.5 %collective-permute-start.6 = (bf16[1,36,3584]{2,1,0:T(8,128)(2,1)}, bf16[1,36,3584]{2,1,0:T(8,128)(2,1)S(1)}, u32[]{:S(2)}, u32[]{:S(2)}) collective-permute-start(bf16[1,36,3584]{2,1,0:T(8,128)(2,1)} %get-tuple-element.30), channel_id=1, source_target_pairs={{0,18},{2,20},{4,22},{6,24},{8,26},{10,28},{12,30},{14,0},{16,2},{... | collective-permute-start | bytes 774152 | tf_op jit(solution)/shard_map/ppermute | solution.py:52
  115.8 33.1 %collective-permute-start.7 = (bf16[1,36,3584]{2,1,0:T(8,128)(2,1)S(1)}, bf16[1,36,3584]{2,1,0:T(8,128)(2,1)S(1)}, u32[]{:S(2)}, u32[]{:S(2)}) collective-permute-start(bf16[1,36,3584]{2,1,0:T(8,128)(2,1)S(1)} %get-tuple-element.29), channel_id=1, source_target_pairs={{0,16},{2,18},{4,20},{6,22},{8,24},{10,26},{12,28},{14,30},{16,0},... | collective-permute-start | bytes 774152 | tf_op jit(solution)/shard_map/ppermute | solution.py:52
  148.8 13.5 %collective-permute-start.8 = (bf16[1,36,3584]{2,1,0:T(8,128)(2,1)}, bf16[1,36,3584]{2,1,0:T(8,128)(2,1)S(1)}, u32[]{:S(2)}, u32[]{:S(2)}) collective-permute-start(bf16[1,36,3584]{2,1,0:T(8,128)(2,1)} %get-tuple-element.28), channel_id=1, source_target_pairs={{0,14},{2,16},{4,18},{6,20},{8,22},{10,24},{12,26},{14,28},{16,30}... | collective-permute-start | bytes 774152 | tf_op jit(solution)/shard_map/ppermute | solution.py:52
  162.3 7.5 %collective-permute-start.9 = (bf16[1,36,3584]{2,1,0:T(8,128)(2,1)S(1)}, bf16[1,36,3584]{2,1,0:T(8,128)(2,1)S(1)}, u32[]{:S(2)}, u32[]{:S(2)}) collective-permute-start(bf16[1,36,3584]{2,1,0:T(8,128)(2,1)S(1)} %copy-done.6), channel_id=1, source_target_pairs={{0,12},{2,14},{4,16},{6,18},{8,20},{10,22},{12,24},{14,26},{16,28}... | collective-permute-start | bytes 774152 | tf_op jit(solution)/shard_map/ppermute | solution.py:52
  169.9 12.6 %collective-permute-start.10 = (bf16[1,36,3584]{2,1,0:T(8,128)(2,1)S(1)}, bf16[1,36,3584]{2,1,0:T(8,128)(2,1)S(1)}, u32[]{:S(2)}, u32[]{:S(2)}) collective-permute-start(bf16[1,36,3584]{2,1,0:T(8,128)(2,1)S(1)} %copy-done.5), channel_id=1, source_target_pairs={{0,10},{2,12},{4,14},{6,16},{8,18},{10,20},{12,22},{14,24},{16,26}... | collective-permute-start | bytes 774152 | tf_op jit(solution)/shard_map/ppermute | solution.py:52
  188.7 163.6 %all-gather.7.cloned.1.call-start = ((), (), s32[]{:S(2)}) async-start(), calls=%async_computation.8 | async-start | bytes 12386304 | tf_op jit(solution)/shard_map/all_gather | solution.py:89
  304.2 100.4 %reduce-scatter.3.cloned.1.call-start = ((), (), s32[]{:S(2)}) async-start(), calls=%async_computation.5 | async-start | bytes 27525120 | tf_op jit(solution)/shard_map/reduce_scatter | solution.py:97
  352.0 80.8 %reduce-scatter.5.cloned.1.call-start = ((), (), s32[]{:S(2)}) async-start(), calls=%async_computation.6 | async-start | bytes 27525120 | tf_op jit(solution)/shard_map/reduce_scatter | solution.py:98
  410.8 107.5 %all-to-all-start = ((bf16[16,36,3584]{2,1,0:T(8,128)(2,1)}), bf16[16,36,3584]{2,1,0:T(8,128)(2,1)}, u32[]{:S(2)}, u32[]{:S(2)}) async-start(bf16[16,36,3584]{2,1,0:T(8,128)(2,1)} %convert_bitcast_fusion.1), calls=%async_computation.1 | async-start | bytes 9175040 | tf_op jit(solution)/shard_map/all_to_all | solution.py:101
  439.0 84.4 %copy-start.9 = (s32[64,8]{0,1:T(8,128)S(1)}, s32[64,8]{0,1:T(8,128)}, u32[]{:S(2)}) copy-start(s32[64,8]{0,1:T(8,128)} %param.9) | copy-start | bytes 6148
  439.0 84.6 %copy-start.8 = (s32[512]{0:T(512)S(1)}, s32[512]{0:T(512)}, u32[]{:S(2)}) copy-start(s32[512]{0:T(512)} %copy-done.7) | copy-start | bytes 6148
  518.3 106.4 %all-to-all-start.2 = ((bf16[16,36,3584]{2,1,0:T(8,128)(2,1)}), bf16[16,36,3584]{2,1,0:T(8,128)(2,1)}, u32[]{:S(2)}, u32[]{:S(2)}) async-start(bf16[16,36,3584]{2,1,0:T(8,128)(2,1)} %convert_bitcast_fusion), calls=%async_computation.4 | async-start | bytes 9175040 | tf_op jit(solution)/shard_map/all_to_all | solution.py:104
  523.7 9.9 %copy-start.4 = (bf16[1152,512]{1,0:T(8,128)(2,1)S(1)}, bf16[1152,512]{1,0:T(8,128)(2,1)}, u32[]{:S(2)}) copy-start(bf16[1152,512]{1,0:T(8,128)(2,1)} %fusion.17) | copy-start | bytes 3538948
  631.7 16.2 %copy-start.1 = (bf16[64,3584]{1,0:T(8,128)(2,1)S(1)}, bf16[64,3584]{1,0:T(8,128)(2,1)}, u32[]{:S(2)}) copy-start(bf16[64,3584]{1,0:T(8,128)(2,1)} %param.8) | copy-start | bytes 1376260
Sparse Core Ops, SparseCore 0:
  188.8 21.7 all-gather.4
  304.3 20.0 all-gather.6
  352.1 28.2 reduce-scatter.2
  404.6 28.1 reduce-scatter.4
